TPU v7x, 32 devices: a whole 2x2x4 slice. The times are simulated.
32 devices in a mesh: groups: 2 (over x), wide: 16 (over z, y, core).
Axes of the slice: x: 2, y: 2, z: 4, core: 2. Of those that a mesh axis runs over, the one named last changes fastest.
Arguments:
- prefix_hidden: bfloat16 [32, 256, 8192], P(('groups', 'wide')), parts along dimension 0, may hold values from -6 to 6
- prefix_lengths: int32 [32], P(('groups', 'wide')), parts along dimension 0, may hold values from 64 to 256
- action_noise: float32 [32, 50, 32], P(('groups', 'wide')), parts along dimension 0, may hold values from -4 to 4
- prefix_gain: float32 [8192], replicated, may hold values from 0.1 to 1.9
- key_weight: bfloat16 [8192, 512], P('wide'), may hold values from -0.0625 to 0.0625
- value_weight: bfloat16 [8192, 512], P('wide'), may hold values from -0.0625 to 0.0625
- input_weight: float32 [32, 1024], replicated, may hold values from -1 to 1
- expert_gain: float32 [1024], replicated, may hold values from 0.1 to 1.9
- expert_query: bfloat16 [1024, 1024], P('wide'), may hold values from -0.1875 to 0.1875
- expert_key: bfloat16 [1024, 512], P('wide'), may hold values from -5.3125 to 5.3125
- expert_value: bfloat16 [1024, 512], P('wide'), may hold values from -0.1875 to 0.1875
- expert_output: bfloat16 [1024, 1024], P('wide'), may hold values from -0.1875 to 0.1875
- final_gain: float32 [1024], replicated, may hold values from 0.1 to 1.9
- output_weight: bfloat16 [1024, 32], replicated, may hold values from -0.1875 to 0.1875
Outputs:
- actions: float32 [32, 50, 32], P(('groups', 'wide')), parts along dimension 0
There are 2 independent parts, one for each index of `groups`. A program takes and returns all parts, laid end to end along the dimension named above; an argument that names none is the same for every part. Nothing has to cross between parts.
Inputs may be any that keep to these rules, and one draw needn't show every extreme that they name: `prefix_lengths`: positions at or after a sample's length are padding and take no part.
All inputs are finite; a program needn't handle non-finite values.
Results may differ from a plain program's by a relative error of at most 0.0075.
Values may be sent and summed in bfloat16 or wider, within the bound.
A program may use at most 128 MiB of HBM per device.

v0:
```python
import jax
import jax.numpy as jnp
from jax import lax
from jax.sharding import PartitionSpec as P

HEAD = 128
STEPS = 4
rope_base = 1000000.0
norm_eps = 1e-06


def normalize(values, norm_gain):
    mean_square = jnp.mean(values * values, axis=-1, keepdims=True)
    return values * lax.rsqrt(mean_square + norm_eps) * norm_gain


def rotate(values, positions):
    half_width = values.shape[-1] // 2
    inv_freqs = rope_base ** (-jnp.arange(half_width, dtype=jnp.float32) * 2.0 / values.shape[-1])
    angles = positions[:, None] * inv_freqs[None, :]
    cosine = jnp.cos(angles)[:, None, :]
    sine_part = jnp.sin(angles)[:, None, :]
    first_half = values[..., :half_width]
    second = values[..., half_width:]
    return jnp.concatenate(
        [first_half * cosine - second * sine_part, second * cosine + first_half * sine_part], -1
    )


def time_embedding(time_value, embed_width):
    half_width = embed_width // 2
    fraction = jnp.arange(half_width, dtype=jnp.float32) / (half_width - 1)
    period = 0.004 * (4.0 / 0.004) ** fraction
    angles = time_value * (2.0 * jnp.pi) / period
    return jnp.concatenate([jnp.sin(angles), jnp.cos(angles)])


def attend(queries, key_cache, value_cache, action_keys, action_values, is_valid):
    span_rows = queries.shape[0]
    groups = key_cache.shape[1] // HEAD
    group_ratio = queries.shape[1] // key_cache.shape[1]
    query_heads = queries.reshape(span_rows, groups, group_ratio, HEAD)
    prefix_keys = key_cache.reshape(-1, groups, HEAD)
    prefix_values = value_cache.reshape(-1, groups, HEAD)
    own_keys = action_keys.reshape(span_rows, groups, HEAD)
    own_values = action_values.reshape(span_rows, groups, HEAD)
    prefix_scores = jnp.einsum(
        "cgrh,pgh->grcp", query_heads, prefix_keys, preferred_element_type=jnp.float32
    )
    prefix_scores = jnp.where(is_valid[None, None, None, :], prefix_scores, -1e30)
    own_scores = jnp.einsum(
        "cgrh,ngh->grcn", query_heads, own_keys, preferred_element_type=jnp.float32
    )
    row_max = jnp.maximum(jnp.max(prefix_scores, -1), jnp.max(own_scores, -1))[..., None]
    prefix_exp = jnp.exp(prefix_scores - row_max)
    own_exp = jnp.exp(own_scores - row_max)
    prob_total = jnp.sum(prefix_exp, -1, keepdims=True) + jnp.sum(own_exp, -1, keepdims=True)
    prefix_prob = (prefix_exp / prob_total).astype(jnp.bfloat16)
    own_prob = (own_exp / prob_total).astype(jnp.bfloat16)
    attn_mixed = jnp.einsum(
        "grcp,pgh->cgrh", prefix_prob, prefix_values, preferred_element_type=jnp.float32
    )
    attn_mixed = attn_mixed + jnp.einsum(
        "grcn,ngh->cgrh", own_prob, own_values, preferred_element_type=jnp.float32
    )
    return attn_mixed.reshape(span_rows, -1).astype(jnp.bfloat16)


def expert_steps(
    noise_rows,
    length,
    input_weight,
    expert_gain,
    query_w,
    key_w,
    value_w,
    output_w,
    final_gain,
    output_weight,
    key_cache,
    value_cache,
):
    span_rows = noise_rows.shape[0]
    is_valid = jnp.arange(key_cache.shape[0], dtype=jnp.int32) < length
    positions = length.astype(jnp.float32) + jnp.arange(span_rows, dtype=jnp.float32)
    action_state = noise_rows
    for step_idx in range(STEPS):
        time_value = 1.0 - step_idx / STEPS
        hidden = jnp.dot(
            action_state,
            input_weight,
            precision=lax.Precision.HIGHEST,
            preferred_element_type=jnp.float32,
        )
        hidden = hidden + time_embedding(time_value, input_weight.shape[1])[None, :]
        normed = normalize(hidden, expert_gain).astype(jnp.bfloat16)
        raw_queries = jnp.dot(normed, query_w, preferred_element_type=jnp.float32)
        queries = rotate(raw_queries.reshape(span_rows, -1, HEAD), positions).reshape(span_rows, -1)
        queries = (queries * HEAD ** (-0.5)).astype(jnp.bfloat16)
        raw_keys = jnp.dot(normed, key_w, preferred_element_type=jnp.float32)
        action_keys = (
            rotate(raw_keys.reshape(span_rows, -1, HEAD), positions)
            .reshape(span_rows, -1)
            .astype(jnp.bfloat16)
        )
        action_values = jnp.dot(normed, value_w, preferred_element_type=jnp.float32).astype(
            jnp.bfloat16
        )
        attn_mixed = attend(queries, key_cache, value_cache, action_keys, action_values, is_valid)
        hidden = hidden + jnp.dot(attn_mixed, output_w, preferred_element_type=jnp.float32)
        final_normed = normalize(hidden, final_gain).astype(jnp.bfloat16)
        velocity = jnp.dot(final_normed, output_weight, preferred_element_type=jnp.float32)
        action_state = action_state - velocity / STEPS
    return action_state


def shards(
    prefix_hidden,
    prefix_lengths,
    action_noise,
    prefix_gain,
    key_weight,
    value_weight,
    input_weight,
    expert_gain,
    expert_query,
    expert_key,
    expert_value,
    expert_output,
    final_gain,
    output_weight,
):
    gathered = (
        lax.all_gather(expert_query, "wide", axis=0, tiled=True),
        lax.all_gather(expert_key, "wide", axis=0, tiled=True),
        lax.all_gather(expert_value, "wide", axis=0, tiled=True),
        lax.all_gather(expert_output, "wide", axis=0, tiled=True),
    )
    hidden = prefix_hidden[0]
    row_count = hidden.shape[0]
    normed = normalize(hidden.astype(jnp.float32), prefix_gain).astype(jnp.bfloat16)
    stacked = jnp.stack([key_weight, value_weight], 0)
    projected = jnp.einsum(
        "pd,kdc->pkc",
        normed,
        lax.all_gather(stacked, "wide", axis=1, tiled=True),
        preferred_element_type=jnp.float32,
    )
    positions = jnp.arange(row_count, dtype=jnp.float32)
    key_cache = (
        rotate(projected[:, 0].reshape(row_count, -1, HEAD), positions)
        .reshape(row_count, -1)
        .astype(jnp.bfloat16)
    )
    value_cache = projected[:, 1].astype(jnp.bfloat16)
    query_w, key_w, value_w, output_w = gathered
    action_state = expert_steps(
        action_noise[0],
        prefix_lengths[0],
        input_weight,
        expert_gain,
        query_w,
        key_w,
        value_w,
        output_w,
        final_gain,
        output_weight,
        key_cache,
        value_cache,
    )
    return action_state[None]


def solution(mesh):
    placed = (
        P(("groups", "wide"), None, None),
        P(("groups", "wide")),
        P(("groups", "wide"), None, None),
        P(),
        P("wide", None),
        P("wide", None),
        P(),
        P(),
        P("wide", None),
        P("wide", None),
        P("wide", None),
        P("wide", None),
        P(),
        P(),
    )
    return jax.shard_map(
        shards,
        mesh=mesh,
        in_specs=placed,
        out_specs=P(("groups", "wide"), None, None),
        check_vma=False,
    )
```

profile of v0, /device:TPU:0, one launch (start us, length us, event | category | flops | bytes accessed | tf_op | source)
XLA Modules:
  0.0 368.0 jit_solution(7898720133912089493)
XLA Ops:
  6.5 0.7 all-gather.10.cloned.1.call-update
  7.3 0.7 all-gather.12.cloned.1.call-update
  8.1 0.7 all-gather.8.cloned.1.call-update
  8.8 2.3 pad_maximum_fusion
  11.1 0.5 all-gather.14.cloned.1.call-update
  12.0 3.1 fusion
  15.1 0.5 fusion.47
  17.1 0.6 pad_maximum_fusion.2
  17.7 0.6 pad_maximum_fusion.3
  18.3 0.6 pad_maximum_fusion.4
  19.0 31.2 %all-gather.10.cloned.1.call-done = bf16[1024,512]{1,0:T(8,128)(2,1)} async-done(((bf16[64,512]{1,0:T(8,128)(2,1)}), bf16[1024,512]{1,0:T(8,128)(2,1)}) %all-gather.10.cloned.1.call-update) | async-done | bytes 1048592 | tf_op jit(solution)/shard_map/all_gather | solution.py:135
  50.2 1.5 fusion.107
  51.9 37.4 %all-gather.12.cloned.1.call-done = bf16[1024,512]{1,0:T(8,128)(2,1)} async-done(((bf16[64,512]{1,0:T(8,128)(2,1)}), bf16[1024,512]{1,0:T(8,128)(2,1)}) %all-gather.12.cloned.1.call-update) | async-done | bytes 1048592 | tf_op jit(solution)/shard_map/all_gather | solution.py:136
  89.2 1.5 convolution_convert_fusion.3
  90.7 0.6 reshape.309
  91.4 40.4 %all-gather.8.cloned.1.call-done = bf16[1024,1024]{1,0:T(8,128)(2,1)} async-done(((bf16[64,1024]{1,0:T(8,128)(2,1)}), bf16[1024,1024]{1,0:T(8,128)(2,1)}) %all-gather.8.cloned.1.call-update) | async-done | bytes 2097168 | tf_op jit(solution)/shard_map/all_gather | solution.py:134
  131.9 2.1 fusion.106
  134.6 124.5 %all-gather.6.cloned.1.call-done = bf16[2,8192,512]{2,1,0:T(8,128)(2,1)} async-done(((bf16[2,512,512]{2,1,0:T(8,128)(2,1)}), bf16[2,8192,512]{2,1,0:T(8,128)(2,1)}) %all-gather.6.cloned.1.call-update) | async-done | bytes 16777232 | tf_op jit(solution)/shard_map/all_gather | solution.py:146
  259.1 9.5 %fusion.4 = f32[256,2,512]{2,0,1:T(8,128)S(1)} fusion(bf16[2,8192,512]{2,1,0:T(8,128)(2,1)} %all-gather.6.cloned.1.call-done, bf16[1,256,8192]{2,1,0:T(8,128)(2,1)} %param.14, f32[8192]{0:T(1024)S(1)} %copy-done.58, f32[256]{0:T(256)S(1)} %add_rsqrt_fusion), kind=kOutput, calls=%fused_computation.6 | convolution fusion | flops 4303355904 | bytes 22053888 | tf_op jit(solution)/shard_map/pd,kdc->pkc/dot_general | solution.py:143
  271.2 29.5 %all-gather.14.cloned.1.call-done = bf16[1024,1024]{1,0:T(8,128)(2,1)} async-done(((bf16[64,1024]{1,0:T(8,128)(2,1)}), bf16[1024,1024]{1,0:T(8,128)(2,1)}) %all-gather.14.cloned.1.call-update) | async-done | bytes 2097168 | tf_op jit(solution)/shard_map/all_gather | solution.py:137
  300.8 2.2 multiply_reduce_fusion.6
  303.9 0.6 copy-done.21
  305.3 0.6 copy-done.34
  306.0 1.7 fusion.100
  307.7 0.9 fusion.109
  308.6 1.6 reshape.311
  310.2 1.1 fusion.96
  311.3 0.8 subtract_convert_fusion.3
  312.1 1.2 fusion.101
  313.3 0.7 max.29
  314.1 1.3 fusion.27
  315.5 2.1 fusion.31
  317.6 0.9 convolution_convert_fusion.2
  318.5 1.5 reshape.312
  320.0 1.3 fusion.19
  321.3 0.7 copy.50
  322.0 1.6 convert_element_type.174
  323.6 2.2 multiply_reduce_fusion.4
  326.7 0.7 copy-done.22
  328.4 0.6 copy-done.35
  329.0 1.1 fusion.102
  330.1 0.9 fusion.111
  331.1 1.6 reshape.314
  332.6 1.1 fusion.95
  333.7 0.8 subtract_convert_fusion.2
  334.5 1.2 fusion.103
  335.7 1.4 fusion.28
  337.2 2.1 fusion.32
  339.3 0.9 convolution_convert_fusion.1
  340.2 1.5 reshape.315
  341.7 1.3 fusion.18
  343.0 0.7 copy.57
  343.7 1.6 convert_element_type.184
  345.3 2.2 multiply_reduce_fusion.2
  347.6 1.0 fusion.23
  348.6 1.2 multiply_reduce_fusion.1
  349.8 0.7 copy-done.19
  350.5 0.8 multiply_convert_fusion.1
  354.5 2.3 fusion.33
  356.7 0.9 convolution_convert_fusion
  357.7 0.9 reshape.318
  358.5 1.3 fusion.17
  360.0 0.6 multiply_reduce_fusion
  360.6 0.8 fusion.22
  (205 shorter events, 11.1 us)
Async XLA Ops:
  6.5 9.1 %copy-start = (f32[32,1024]{1,0:T(8,128)S(1)}, f32[32,1024]{1,0:T(8,128)}, u32[]{:S(2)}) copy-start(f32[32,1024]{1,0:T(8,128)} %param.20) | copy-start | bytes 393220
  6.5 43.7 %all-gather.10.cloned.1.call-start = ((), (), s32[]{:S(2)}) async-start(), calls=%async_computation.2 | async-start | bytes 1114112 | tf_op jit(solution)/shard_map/all_gather | solution.py:135
  7.3 82.0 %all-gather.12.cloned.1.call-start = ((), (), s32[]{:S(2)}) async-start(), calls=%async_computation.3 | async-start | bytes 1114112 | tf_op jit(solution)/shard_map/all_gather | solution.py:136
  8.0 123.8 %all-gather.8.cloned.1.call-start = ((), (), s32[]{:S(2)}) async-start(), calls=%async_computation.1 | async-start | bytes 2228224 | tf_op jit(solution)/shard_map/all_gather | solution.py:134
  8.7 250.4 %all-gather.6.cloned.1.call-start = ((), (), s32[]{:S(2)}) async-start(), calls=%async_computation | async-start | bytes 17825792 | tf_op jit(solution)/shard_map/all_gather | solution.py:146
  11.1 289.7 %all-gather.14.cloned.1.call-start = ((), (), s32[]{:S(2)}) async-start(), calls=%async_computation.4 | async-start | bytes 2228224 | tf_op jit(solution)/shard_map/all_gather | solution.py:137
  11.9 3.7 %copy-start.44 = (f32[1,50,32]{1,2,0:T(8,128)S(1)}, f32[1,50,32]{1,2,0:T(8,128)}, u32[]{:S(2)}) copy-start(f32[1,50,32]{1,2,0:T(8,128)} %param.16) | copy-start | bytes 19204
  12.0 6.9 %copy-start.41 = (f32[1024]{0:T(1024)S(1)}, f32[1024]{0:T(1024)}, u32[]{:S(2)}) copy-start(f32[1024]{0:T(1024)} %param.21) | copy-start | bytes 12292
  16.1 117.8 %copy-start.17 = (f32[50,1024]{1,0:T(8,128)}, f32[50,1024]{1,0:T(8,128)S(1)}, u32[]{:S(2)}) copy-start(f32[50,1024]{1,0:T(8,128)S(1)} %get-tuple-element.38) | copy-start | bytes 614404
  17.0 117.0 %copy-start.7 = (f32[50,64]{1,0:T(8,128)}, f32[50,64]{1,0:T(8,128)S(1)}, u32[]{:S(2)}) copy-start(f32[50,64]{1,0:T(8,128)S(1)} %get-tuple-element.33) | copy-start | bytes 38404
  17.0 117.0 %copy-start.12 = (f32[50,64]{1,0:T(8,128)}, f32[50,64]{1,0:T(8,128)S(1)}, u32[]{:S(2)}) copy-start(f32[50,64]{1,0:T(8,128)S(1)} %get-tuple-element.34) | copy-start | bytes 38404
  17.0 252.6 %copy-start.53 = (pred[256]{0:T(512)(128)(4,1)}, pred[256]{0:T(512)(128)(4,1)S(1)}, u32[]{:S(2)}) copy-start(pred[256]{0:T(512)(128)(4,1)S(1)} %iota_compare_fusion) | copy-start | bytes 772
  91.4 167.7 %copy-start.58 = (f32[8192]{0:T(1024)S(1)}, f32[8192]{0:T(1024)}, u32[]{:S(2)}) copy-start(f32[8192]{0:T(1024)} %param.17) | copy-start | bytes 98308
  269.0 1.4 copy-start.39
  269.7 1.1 copy-start.49
  270.1 30.6 %copy-start.18 = (f32[50,1024]{1,0:T(8,128)S(1)}, f32[50,1024]{1,0:T(8,128)}, u32[]{:S(2)}) copy-start(f32[50,1024]{1,0:T(8,128)} %copy-done.17) | copy-start | bytes 614404
  270.8 32.2 %copy-start.30 = (bf16[1024,32]{0,1:T(8,128)(2,1)S(1)}, bf16[1024,32]{0,1:T(8,128)(2,1)}, u32[]{:S(2)}) copy-start(bf16[1024,32]{0,1:T(8,128)(2,1)} %param.27) | copy-start | bytes 196612
  270.8 32.2 %copy-start.45 = (f32[1,50,32]{1,2,0:T(8,128)S(1)}, f32[1,50,32]{1,2,0:T(8,128)}, u32[]{:S(2)}) copy-start(f32[1,50,32]{1,2,0:T(8,128)} %param.16) | copy-start | bytes 19204
  270.8 32.2 %copy-start.46 = (f32[1024]{0:T(1024)S(1)}, f32[1024]{0:T(1024)}, u32[]{:S(2)}) copy-start(f32[1024]{0:T(1024)} %param.26) | copy-start | bytes 12292
  270.8 32.4 %copy-start.52 = (f32[1024]{0:T(1024)S(1)}, f32[1024]{0:T(1024)}, u32[]{:S(2)}) copy-start(f32[1024]{0:T(1024)} %pad_maximum_fusion.2) | copy-start | bytes 12292
  271.1 32.7 %copy-start.42 = (f32[1024]{0:T(1024)S(1)}, f32[1024]{0:T(1024)}, u32[]{:S(2)}) copy-start(f32[1024]{0:T(1024)} %param.21) | copy-start | bytes 12292
  271.1 33.4 %copy-start.1 = (bf16[1024,1024]{1,0:T(8,128)(2,1)S(1)}, bf16[1024,1024]{1,0:T(8,128)(2,1)}, u32[]{:S(2)}) copy-start(bf16[1024,1024]{1,0:T(8,128)(2,1)} %all-gather.8.cloned.1.call-done) | copy-start | bytes 6291460
  303.2 1.8 copy-start.8
  303.2 1.8 copy-start.13
  303.7 0.7 copy-start.21
  304.4 3.2 copy-start.25
  304.4 1.5 copy-start.54
  304.9 2.7 copy-start.4
  305.3 0.7 copy-start.34
  310.2 7.4 %copy-start.3 = (bf16[1024,512]{1,0:T(8,128)(2,1)S(1)}, bf16[1024,512]{1,0:T(8,128)(2,1)}, u32[]{:S(2)}) copy-start(bf16[1024,512]{1,0:T(8,128)(2,1)} %all-gather.12.cloned.1.call-done) | copy-start | bytes 3145732
  310.2 7.4 %copy-start.26 = (bf16[50,1024]{1,0:T(8,128)(2,1)S(1)}, bf16[50,1024]{1,0:T(8,128)(2,1)}, u32[]{:S(2)}) copy-start(bf16[50,1024]{1,0:T(8,128)(2,1)} %copy-done.25) | copy-start | bytes 307204
  313.3 2.0 copy-start.37
  314.1 1.4 copy-start.50
  315.4 2.1 copy-start.57
  323.6 2.3 copy-start.31
  323.6 2.3 copy-start.47
  323.6 2.5 copy-start.51
  323.6 3.7 %copy-start.43 = (f32[1024]{0:T(1024)S(1)}, f32[1024]{0:T(1024)}, u32[]{:S(2)}) copy-start(f32[1024]{0:T(1024)} %param.21) | copy-start | bytes 12292
  326.1 1.9 copy-start.40
  326.2 1.9 copy-start.9
  326.2 1.9 copy-start.14
  326.7 0.7 copy-start.22
  327.4 2.7 copy-start.27
  327.5 1.6 copy-start.55
  327.9 2.2 copy-start.5
  328.4 0.7 copy-start.35
  332.6 6.7 %copy-start.28 = (bf16[50,1024]{1,0:T(8,128)(2,1)S(1)}, bf16[50,1024]{1,0:T(8,128)(2,1)}, u32[]{:S(2)}) copy-start(bf16[50,1024]{1,0:T(8,128)(2,1)} %copy-done.27) | copy-start | bytes 307204
  335.7 1.4 copy-start.38
  345.3 2.2 copy-start.32
  348.5 3.3 copy-start.10
  348.5 3.3 copy-start.15
  349.7 0.7 copy-start.19
  351.2 1.3 copy-start.23
  351.2 0.9 copy-start.56
  351.7 1.2 copy-start.6
  351.8 1.6 copy-start.11
  351.9 1.6 copy-start.16
  353.0 1.2 copy-start.29
  353.3 3.4 copy-start.24
  353.8 0.7 copy-start.36
  354.5 5.5 %copy-start.2 = (bf16[1024,1024]{1,0:T(8,128)(2,1)S(1)}, bf16[1024,1024]{1,0:T(8,128)(2,1)}, u32[]{:S(2)}) copy-start(bf16[1024,1024]{1,0:T(8,128)(2,1)} %all-gather.14.cloned.1.call-done) | copy-start | bytes 6291460
  354.5 5.5 %copy-start.20 = (f32[50,1024]{1,0:T(8,128)S(1)}, f32[50,1024]{1,0:T(8,128)}, u32[]{:S(2)}) copy-start(f32[50,1024]{1,0:T(8,128)} %copy-done.19) | copy-start | bytes 614404
  357.6 2.9 copy-start.33
  357.6 2.9 copy-start.48
Sparse Core Ops, SparseCore 0:
  9.5 40.6 all-gather.9
  52.4 36.8 all-gather.11
  91.4 40.4 all-gather.7
  133.9 125.1 all-gather.5
  261.1 39.6 all-gather.13
where the time goes:
time: 369 us; the launch traced here: 368 us
  waiting for transfers between devices  266 us (72%)
  matrix products  50.5 us (14%)
  local copies, waits for them, and re-layouts  20.1 us (5%)
  other arithmetic  16.4 us (4%)
  between operations  15.1 us (4%)
    all_gather x1, waiting for transfers between devices, shards(): lax.all_gather(stacked, 'wide', axis=1, tiled=True)  124 us
    all_gather x1, waiting for transfers between devices, shards(): lax.all_gather(expert_query, 'wide', axis=0, tiled=True)  40.4 us
    all_gather x1, waiting for transfers between devices, shards(): lax.all_gather(expert_value, 'wide', axis=0, tiled=True)  37.4 us
    all_gather x1, waiting for transfers between devices, shards(): lax.all_gather(expert_key, 'wide', axis=0, tiled=True)  31.2 us
    all_gather x1, waiting for transfers between devices, shards(): lax.all_gather(expert_output, 'wide', axis=0, tiled=True)  29.5 us
    dot_general x1, matrix products, shards(): jnp.einsum('pd,kdc->pkc', normed, lax.all_gather(stacked, 'wide', axis=1,...  9.54 us
  transfers between devices with their start and end apart: 5, of which 5 were waited for; matrix products, arithmetic and copies ran while one was open for 7% of the time, Pallas kernels for 0%

commit v1 on v0

--- a/solution.py
+++ b/solution.py
@@ -2,6 +2,7 @@
 import jax.numpy as jnp
 from jax import lax
 from jax.sharding import PartitionSpec as P
+from jax.lax import axis_index, ppermute, psum
 
 HEAD = 128
 STEPS = 4
@@ -140,12 +141,35 @@
     row_count = hidden.shape[0]
     normed = normalize(hidden.astype(jnp.float32), prefix_gain).astype(jnp.bfloat16)
     stacked = jnp.stack([key_weight, value_weight], 0)
+    near, all_values, tmp = (psum(1, "wide"), axis_index("wide"), stacked.shape[1])
+    in_order = [(q, (q + 1) % near) for q in range(near)]
+    sheets = [(q, (q - 1) % near) for q in range(near)]
+    back = near // 2
+    later = built = stacked
     projected = jnp.einsum(
         "pd,kdc->pkc",
-        normed,
-        lax.all_gather(stacked, "wide", axis=1, tiled=True),
+        lax.dynamic_slice_in_dim(normed, all_values * tmp, stacked.shape[1], axis=1),
+        stacked,
         preferred_element_type=jnp.float32,
     )
+    for t in range(1, back + 1):
+        later = ppermute(later, "wide", perm=in_order)
+        if t < near - back:
+            built = ppermute(built, axis_name="wide", perm=sheets)
+            projected = projected + jnp.einsum(
+                "pd,kdc->pkc",
+                lax.dynamic_slice_in_dim(
+                    normed, (all_values + t) % near * tmp, built.shape[1], axis=1
+                ),
+                built,
+                preferred_element_type=jnp.float32,
+            )
+        projected = projected + jnp.einsum(
+            "pd,kdc->pkc",
+            lax.dynamic_slice_in_dim(normed, (all_values - t) % near * tmp, later.shape[1], axis=1),
+            later,
+            preferred_element_type=jnp.float32,
+        )
     positions = jnp.arange(row_count, dtype=jnp.float32)
     key_cache = (
         rotate(projected[:, 0].reshape(row_count, -1, HEAD), positions)

time: 369 us -> 318 us (0.86)
  the two profiles are of different devices: /device:TPU:0 before, /device:TPU:1 now
where the time goes in v1:
time: 318 us; the launch traced here: 317 us
  waiting for transfers between devices  173 us (54%)
  matrix products  64.4 us (20%)
  local copies, waits for them, and re-layouts  25.1 us (8%)
  other arithmetic  20.1 us (6%)
  starting transfers between devices  18.9 us (6%)
  between operations  15.1 us (5%)
    ppermute x8, waiting for transfers between devices, shards(): later = ppermute(later, 'wide', perm=in_order)  80.5 us
    ppermute x7, waiting for transfers between devices, shards(): built = ppermute(built, axis_name='wide', perm=sheets)  56.2 us
    all_gather x1, waiting for transfers between devices, shards(): lax.all_gather(expert_query, 'wide', axis=0, tiled=True)  19.6 us
    ppermute x8, starting transfers between devices, shards(): later = ppermute(later, 'wide', perm=in_order)  18 us
    all_gather x1, waiting for transfers between devices, shards(): lax.all_gather(expert_value, 'wide', axis=0, tiled=True)  14.8 us
    dot_general x8, matrix products, shards(): jnp.einsum('pd,kdc->pkc', lax.dynamic_slice_in_dim(normed, (all_values -...  11.1 us
    dot_general x4, matrix products, expert_steps(): jnp.dot(attn_mixed, output_w, preferred_element_type=jnp.float32)  8.07 us
    convert_element_type x8, local copies, waits for them, and re-layouts, attend(): return attn_mixed.reshape(span_rows, -1).astype(jnp.bfloat16)  7.03 us
  transfers between devices with their start and end apart: 19, of which 11 were waited for; matrix products, arithmetic and copies ran while one was open for 14% of the time, Pallas kernels for 0%

profile of v1, /device:TPU:1, one launch (start us, length us, event | category | flops | bytes accessed | tf_op | source)
XLA Modules:
  0.0 316.7 jit_solution(9807925506747875978)
XLA Ops:
  8.8 1.3 pad_maximum_fusion
  10.2 2.7 collective-permute-start.1
  12.9 3.3 %fusion = f32[256]{0:T(256)S(1)} fusion(bf16[1,256,8192]{2,1,0:T(8,128)(2,1)} %param.14), kind=kLoop, calls=%fused_computation.2 | loop fusion | flops 6291200 | bytes 4195328 | tf_op jit(solution)/shard_map/reduce_sum | solution.py:14
  16.3 3.2 fusion.2
  20.2 16.3 %collective-permute-done.1 = bf16[2,512,512]{2,1,0:T(8,128)(2,1)} collective-permute-done((bf16[2,512,512]{2,1,0:T(8,128)(2,1)S(1)}, bf16[2,512,512]{2,1,0:T(8,128)(2,1)}, u32[]{:S(2)}, u32[]{:S(2)}) %collective-permute-start.1) | collective-permute-done | bytes 1048608 | tf_op jit(solution)/shard_map/ppermute | solution.py:156
  36.5 2.6 collective-permute-start.3
  41.7 23.5 %collective-permute-done.3 = bf16[2,512,512]{2,1,0:T(8,128)(2,1)S(1)} collective-permute-done((bf16[2,512,512]{2,1,0:T(8,128)(2,1)}, bf16[2,512,512]{2,1,0:T(8,128)(2,1)S(1)}, u32[]{:S(2)}, u32[]{:S(2)}) %collective-permute-start.3) | collective-permute-done | bytes 1048608 | tf_op jit(solution)/shard_map/ppermute | solution.py:156
  65.2 2.4 collective-permute-start.5
  67.6 1.7 fusion.51
  69.5 1.2 fusion.86
  70.8 4.6 %collective-permute-done.2 = bf16[2,512,512]{2,1,0:T(8,128)(2,1)S(1)} collective-permute-done((bf16[2,512,512]{2,1,0:T(8,128)(2,1)S(1)}, bf16[2,512,512]{2,1,0:T(8,128)(2,1)S(1)}, u32[]{:S(2)}, u32[]{:S(2)}) %collective-permute-start.2) | collective-permute-done | bytes 1048608 | tf_op jit(solution)/shard_map/ppermute | solution.py:158
  75.4 15.8 %collective-permute-done.5 = bf16[2,512,512]{2,1,0:T(8,128)(2,1)} collective-permute-done((bf16[2,512,512]{2,1,0:T(8,128)(2,1)S(1)}, bf16[2,512,512]{2,1,0:T(8,128)(2,1)}, u32[]{:S(2)}, u32[]{:S(2)}) %collective-permute-start.5) | collective-permute-done | bytes 1048608 | tf_op jit(solution)/shard_map/ppermute | solution.py:156
  91.3 2.6 collective-permute-start.7
  93.9 1.4 convolution_add_fusion.8
  95.2 1.8 convolution_add_fusion.7
  97.0 1.5 fusion.162
  98.6 14.8 %all-gather.9.cloned.1.call-done = bf16[1024,512]{1,0:T(8,128)(2,1)} async-done(((bf16[64,512]{1,0:T(8,128)(2,1)}), bf16[1024,512]{1,0:T(8,128)(2,1)}) %all-gather.9.cloned.1.call-update) | async-done | bytes 1048592 | tf_op jit(solution)/shard_map/all_gather | solution.py:137
  113.3 1.5 convolution_convert_fusion.3
  115.9 1.5 collective-permute-start.9
  118.1 1.7 fusion.46
  119.8 1.4 fusion.8
  121.2 21.4 %collective-permute-done.6 = bf16[2,512,512]{2,1,0:T(8,128)(2,1)S(1)} collective-permute-done((bf16[2,512,512]{2,1,0:T(8,128)(2,1)}, bf16[2,512,512]{2,1,0:T(8,128)(2,1)S(1)}, u32[]{:S(2)}, u32[]{:S(2)}) %collective-permute-start.6) | collective-permute-done | bytes 1048608 | tf_op jit(solution)/shard_map/ppermute | solution.py:158
  142.6 1.7 fusion.43
  144.3 9.0 %collective-permute-done.9 = bf16[2,512,512]{2,1,0:T(8,128)(2,1)} collective-permute-done((bf16[2,512,512]{2,1,0:T(8,128)(2,1)}, bf16[2,512,512]{2,1,0:T(8,128)(2,1)}, u32[]{:S(2)}, u32[]{:S(2)}) %collective-permute-start.9) | collective-permute-done | bytes 1048608 | tf_op jit(solution)/shard_map/ppermute | solution.py:156
  153.4 2.5 collective-permute-start.11
  155.8 1.8 fusion.7
  157.6 19.6 %all-gather.5.cloned.1.call-done = bf16[1024,1024]{1,0:T(8,128)(2,1)} async-done(((bf16[64,1024]{1,0:T(8,128)(2,1)}), bf16[1024,1024]{1,0:T(8,128)(2,1)}) %all-gather.5.cloned.1.call-update) | async-done | bytes 2097168 | tf_op jit(solution)/shard_map/all_gather | solution.py:135
  177.2 2.2 fusion.161
  181.1 1.5 collective-permute-start.13
  182.6 1.7 fusion.40
  184.7 1.7 fusion.37
  186.4 20.3 %collective-permute-done.10 = bf16[2,512,512]{2,1,0:T(8,128)(2,1)S(1)} collective-permute-done((bf16[2,512,512]{2,1,0:T(8,128)(2,1)S(1)}, bf16[2,512,512]{2,1,0:T(8,128)(2,1)S(1)}, u32[]{:S(2)}, u32[]{:S(2)}) %collective-permute-start.10) | collective-permute-done | bytes 1048608 | tf_op jit(solution)/shard_map/ppermute | solution.py:158
  207.2 15.8 %collective-permute-done.13 = bf16[2,512,512]{2,1,0:T(8,128)(2,1)S(1)} collective-permute-done((bf16[2,512,512]{2,1,0:T(8,128)(2,1)}, bf16[2,512,512]{2,1,0:T(8,128)(2,1)S(1)}, u32[]{:S(2)}, u32[]{:S(2)}) %collective-permute-start.13) | collective-permute-done | bytes 1048608 | tf_op jit(solution)/shard_map/ppermute | solution.py:156
  223.0 2.4 collective-permute-start.14
  225.4 1.7 fusion.34
  227.9 9.9 %collective-permute-done.12 = bf16[2,512,512]{2,1,0:T(8,128)(2,1)S(1)} collective-permute-done((bf16[2,512,512]{2,1,0:T(8,128)(2,1)S(1)}, bf16[2,512,512]{2,1,0:T(8,128)(2,1)S(1)}, u32[]{:S(2)}, u32[]{:S(2)}) %collective-permute-start.12) | collective-permute-done | bytes 1048608 | tf_op jit(solution)/shard_map/ppermute | solution.py:158
  242.6 1.6 convert_element_type.164
  244.2 2.2 multiply_reduce_fusion.6
  246.4 1.1 fusion.25
  247.4 1.2 multiply_reduce_fusion.5
  252.8 1.5 fusion.163
  260.6 1.5 reshape.312
  262.0 1.3 fusion.19
  264.1 1.6 convert_element_type.174
  265.6 2.2 multiply_reduce_fusion.4
  267.8 1.1 fusion.24
  269.0 1.2 multiply_reduce_fusion.3
  272.3 2.1 fusion.166
  274.4 1.6 reshape.314
  276.0 1.1 fusion.150
  277.1 1.4 fusion.165
  279.7 1.1 fusion.157
  284.1 1.5 reshape.315
  285.5 1.3 fusion.18
  287.6 1.6 convert_element_type.184
  289.2 2.2 multiply_reduce_fusion.2
  291.4 1.1 fusion.23
  292.4 1.2 multiply_reduce_fusion.1
  295.8 2.2 fusion.168
  297.9 1.6 reshape.317
  299.5 1.1 fusion.149
  300.6 1.4 fusion.167
  306.3 1.3 fusion.17
  307.8 1.5 multiply_reduce_fusion
  (228 shorter events, 40.4 us)
Async XLA Ops:
  6.5 34.6 %copy-start = (f32[32,1024]{1,0:T(8,128)S(1)}, f32[32,1024]{1,0:T(8,128)}, u32[]{:S(2)}) copy-start(f32[32,1024]{1,0:T(8,128)} %param.20) | copy-start | bytes 393220
  6.5 9.6 %copy-start.45 = (f32[8192]{0:T(1024)S(1)}, f32[8192]{0:T(1024)}, u32[]{:S(2)}) copy-start(f32[8192]{0:T(1024)} %param.17) | copy-start | bytes 98308
  6.5 90.5 %all-gather.7.cloned.1.call-start = ((), (), s32[]{:S(2)}) async-start(), calls=%async_computation.1 | async-start | bytes 1114112 | tf_op jit(solution)/shard_map/all_gather | solution.py:136
  7.3 106.1 %all-gather.9.cloned.1.call-start = ((), (), s32[]{:S(2)}) async-start(), calls=%async_computation.2 | async-start | bytes 1114112 | tf_op jit(solution)/shard_map/all_gather | solution.py:137
  8.0 169.2 %all-gather.5.cloned.1.call-start = ((), (), s32[]{:S(2)}) async-start(), calls=%async_computation | async-start | bytes 2228224 | tf_op jit(solution)/shard_map/all_gather | solution.py:135
  8.7 235.4 %all-gather.11.cloned.1.call-start = ((), (), s32[]{:S(2)}) async-start(), calls=%async_computation.3 | async-start | bytes 2228224 | tf_op jit(solution)/shard_map/all_gather | solution.py:138
  10.1 31.5 %collective-permute-start = (bf16[2,512,512]{2,1,0:T(8,128)(2,1)S(1)}, bf16[2,512,512]{2,1,0:T(8,128)(2,1)S(1)}, u32[]{:S(2)}, u32[]{:S(2)}) collective-permute-start(bf16[2,512,512]{2,1,0:T(8,128)(2,1)S(1)} %pad_maximum_fusion), channel_id=1, source_target_pairs={{0,15},{1,0},{2,1},{3,2},{4,3},{5,4},{6,5},{7,6},{8,7},{9,8},{10,9... | collective-permute-start | bytes 3145736 | tf_op jit(solution)/shard_map/ppermute | solution.py:158
  10.2 26.3 %collective-permute-start.1 = (bf16[2,512,512]{2,1,0:T(8,128)(2,1)S(1)}, bf16[2,512,512]{2,1,0:T(8,128)(2,1)}, u32[]{:S(2)}, u32[]{:S(2)}) collective-permute-start(bf16[2,512,512]{2,1,0:T(8,128)(2,1)S(1)} %pad_maximum_fusion), channel_id=1, source_target_pairs={{0,1},{1,2},{2,3},{3,4},{4,5},{5,6},{6,7},{7,8},{8,9},{9,10},{10,1... | collective-permute-start | bytes 3145736 | tf_op jit(solution)/shard_map/ppermute | solution.py:156
  12.9 3.5 %copy-start.5 = (bf16[1,256,8192]{2,1,0:T(8,128)(2,1)S(1)}, bf16[1,256,8192]{2,1,0:T(8,128)(2,1)}, u32[]{:S(2)}) copy-start(bf16[1,256,8192]{2,1,0:T(8,128)(2,1)} %param.14) | copy-start | bytes 12582916
  16.3 24.8 %copy-start.41 = (f32[1,50,32]{1,2,0:T(8,128)S(1)}, f32[1,50,32]{1,2,0:T(8,128)}, u32[]{:S(2)}) copy-start(f32[1,50,32]{1,2,0:T(8,128)} %param.16) | copy-start | bytes 19204
  16.3 54.4 %copy-start.40 = (f32[1024]{0:T(1024)S(1)}, f32[1024]{0:T(1024)}, u32[]{:S(2)}) copy-start(f32[1024]{0:T(1024)} %param.21) | copy-start | bytes 12292
  36.5 28.7 %collective-permute-start.3 = (bf16[2,512,512]{2,1,0:T(8,128)(2,1)}, bf16[2,512,512]{2,1,0:T(8,128)(2,1)S(1)}, u32[]{:S(2)}, u32[]{:S(2)}) collective-permute-start(bf16[2,512,512]{2,1,0:T(8,128)(2,1)} %collective-permute-done.1), channel_id=1, source_target_pairs={{0,1},{1,2},{2,3},{3,4},{4,5},{5,6},{6,7},{7,8},{8,9},{9,10},{10,1... | collective-permute-start | bytes 3145736 | tf_op jit(solution)/shard_map/ppermute | solution.py:156
  39.1 201.4 %copy-start.46 = (pred[256]{0:T(512)(128)(4,1)}, pred[256]{0:T(512)(128)(4,1)S(1)}, u32[]{:S(2)}) copy-start(pred[256]{0:T(512)(128)(4,1)S(1)} %iota_compare_fusion) | copy-start | bytes 772
  41.6 49.7 %copy-start.13 = (f32[50,1024]{1,0:T(8,128)}, f32[50,1024]{1,0:T(8,128)S(1)}, u32[]{:S(2)}) copy-start(f32[50,1024]{1,0:T(8,128)S(1)} %get-tuple-element.38) | copy-start | bytes 614404
  41.6 33.8 %collective-permute-start.2 = (bf16[2,512,512]{2,1,0:T(8,128)(2,1)S(1)}, bf16[2,512,512]{2,1,0:T(8,128)(2,1)S(1)}, u32[]{:S(2)}, u32[]{:S(2)}) collective-permute-start(bf16[2,512,512]{2,1,0:T(8,128)(2,1)S(1)} %collective-permute-done), channel_id=1, source_target_pairs={{0,15},{1,0},{2,1},{3,2},{4,3},{5,4},{6,5},{7,6},{8,7},{9,8},{10,9... | collective-permute-start | bytes 3145736 | tf_op jit(solution)/shard_map/ppermute | solution.py:158
  65.2 28.6 %copy-start.23 = (bf16[2,512,512]{2,1,0:T(8,128)(2,1)}, bf16[2,512,512]{2,1,0:T(8,128)(2,1)S(1)}, u32[]{:S(2)}) copy-start(bf16[2,512,512]{2,1,0:T(8,128)(2,1)S(1)} %collective-permute-done.3) | copy-start | bytes 3145732
  65.2 26.1 %collective-permute-start.5 = (bf16[2,512,512]{2,1,0:T(8,128)(2,1)S(1)}, bf16[2,512,512]{2,1,0:T(8,128)(2,1)}, u32[]{:S(2)}, u32[]{:S(2)}) collective-permute-start(bf16[2,512,512]{2,1,0:T(8,128)(2,1)S(1)} %collective-permute-done.3), channel_id=1, source_target_pairs={{0,1},{1,2},{2,3},{3,4},{4,5},{5,6},{6,7},{7,8},{8,9},{9,10},{10,1... | collective-permute-start | bytes 3145736 | tf_op jit(solution)/shard_map/ppermute | solution.py:156
  69.5 110.0 %copy-start.7 = (f32[50,64]{1,0:T(8,128)}, f32[50,64]{1,0:T(8,128)S(1)}, u32[]{:S(2)}) copy-start(f32[50,64]{1,0:T(8,128)S(1)} %get-tuple-element.33) | copy-start | bytes 38404
  69.5 110.0 %copy-start.10 = (f32[50,64]{1,0:T(8,128)}, f32[50,64]{1,0:T(8,128)S(1)}, u32[]{:S(2)}) copy-start(f32[50,64]{1,0:T(8,128)S(1)} %get-tuple-element.34) | copy-start | bytes 38404
  75.4 40.1 %collective-permute-start.4 = (bf16[2,512,512]{2,1,0:T(8,128)(2,1)S(1)}, bf16[2,512,512]{2,1,0:T(8,128)(2,1)}, u32[]{:S(2)}, u32[]{:S(2)}) collective-permute-start(bf16[2,512,512]{2,1,0:T(8,128)(2,1)S(1)} %collective-permute-done.2), channel_id=1, source_target_pairs={{0,15},{1,0},{2,1},{3,2},{4,3},{5,4},{6,5},{7,6},{8,7},{9,8},{10,9... | collective-permute-start | bytes 3145736 | tf_op jit(solution)/shard_map/ppermute | solution.py:158
  91.3 24.7 %collective-permute-start.7 = (bf16[2,512,512]{2,1,0:T(8,128)(2,1)}, bf16[2,512,512]{2,1,0:T(8,128)(2,1)}, u32[]{:S(2)}, u32[]{:S(2)}) collective-permute-start(bf16[2,512,512]{2,1,0:T(8,128)(2,1)} %collective-permute-done.5), channel_id=1, source_target_pairs={{0,1},{1,2},{2,3},{3,4},{4,5},{5,6},{6,7},{7,8},{8,9},{9,10},{10,1... | collective-permute-start | bytes 3145736 | tf_op jit(solution)/shard_map/ppermute | solution.py:156
  115.5 27.1 %collective-permute-start.6 = (bf16[2,512,512]{2,1,0:T(8,128)(2,1)}, bf16[2,512,512]{2,1,0:T(8,128)(2,1)S(1)}, u32[]{:S(2)}, u32[]{:S(2)}) collective-permute-start(bf16[2,512,512]{2,1,0:T(8,128)(2,1)} %collective-permute-done.4), channel_id=1, source_target_pairs={{0,15},{1,0},{2,1},{3,2},{4,3},{5,4},{6,5},{7,6},{8,7},{9,8},{10,9... | collective-permute-start | bytes 3145736 | tf_op jit(solution)/shard_map/ppermute | solution.py:158
  115.9 37.4 %collective-permute-start.9 = (bf16[2,512,512]{2,1,0:T(8,128)(2,1)}, bf16[2,512,512]{2,1,0:T(8,128)(2,1)}, u32[]{:S(2)}, u32[]{:S(2)}) collective-permute-start(bf16[2,512,512]{2,1,0:T(8,128)(2,1)} %collective-permute-done.7), channel_id=1, source_target_pairs={{0,1},{1,2},{2,3},{3,4},{4,5},{5,6},{6,7},{7,8},{8,9},{9,10},{10,1... | collective-permute-start | bytes 3145736 | tf_op jit(solution)/shard_map/ppermute | solution.py:156
  142.6 37.2 %collective-permute-start.8 = (bf16[2,512,512]{2,1,0:T(8,128)(2,1)S(1)}, bf16[2,512,512]{2,1,0:T(8,128)(2,1)S(1)}, u32[]{:S(2)}, u32[]{:S(2)}) collective-permute-start(bf16[2,512,512]{2,1,0:T(8,128)(2,1)S(1)} %collective-permute-done.6), channel_id=1, source_target_pairs={{0,15},{1,0},{2,1},{3,2},{4,3},{5,4},{6,5},{7,6},{8,7},{9,8},{10,9... | collective-permute-start | bytes 3145736 | tf_op jit(solution)/shard_map/ppermute | solution.py:158
  153.4 27.8 %collective-permute-start.11 = (bf16[2,512,512]{2,1,0:T(8,128)(2,1)}, bf16[2,512,512]{2,1,0:T(8,128)(2,1)}, u32[]{:S(2)}, u32[]{:S(2)}) collective-permute-start(bf16[2,512,512]{2,1,0:T(8,128)(2,1)} %collective-permute-done.9), channel_id=1, source_target_pairs={{0,1},{1,2},{2,3},{3,4},{4,5},{5,6},{6,7},{7,8},{8,9},{9,10},{10,1... | collective-permute-start | bytes 3145736 | tf_op jit(solution)/shard_map/ppermute | solution.py:156
  177.2 3.0 copy-start.38
  177.2 5.4 %copy-start.6 = (bf16[256,8192]{1,0:T(8,128)(2,1)S(1)}, bf16[256,8192]{1,0:T(8,128)(2,1)}, u32[]{:S(2)}) copy-start(bf16[256,8192]{1,0:T(8,128)(2,1)} %fusion.2) | copy-start | bytes 12582916
  179.8 6.6 %copy-start.25 = (bf16[50,8,128]{2,0,1:T(8,128)(2,1)}, bf16[50,8,128]{2,0,1:T(8,128)(2,1)S(1)}, u32[]{:S(2)}) copy-start(bf16[50,8,128]{2,0,1:T(8,128)(2,1)S(1)} %copy.37) | copy-start | bytes 307204
  179.8 26.9 %collective-permute-start.10 = (bf16[2,512,512]{2,1,0:T(8,128)(2,1)S(1)}, bf16[2,512,512]{2,1,0:T(8,128)(2,1)S(1)}, u32[]{:S(2)}, u32[]{:S(2)}) collective-permute-start(bf16[2,512,512]{2,1,0:T(8,128)(2,1)S(1)} %collective-permute-done.8), channel_id=1, source_target_pairs={{0,15},{1,0},{2,1},{3,2},{4,3},{5,4},{6,5},{7,6},{8,7},{9,8},{10,9... | collective-permute-start | bytes 3145736 | tf_op jit(solution)/shard_map/ppermute | solution.py:158
  181.1 41.8 %collective-permute-start.13 = (bf16[2,512,512]{2,1,0:T(8,128)(2,1)}, bf16[2,512,512]{2,1,0:T(8,128)(2,1)S(1)}, u32[]{:S(2)}, u32[]{:S(2)}) collective-permute-start(bf16[2,512,512]{2,1,0:T(8,128)(2,1)} %collective-permute-done.11), channel_id=1, source_target_pairs={{0,1},{1,2},{2,3},{3,4},{4,5},{5,6},{6,7},{7,8},{8,9},{9,10},{10,1... | collective-permute-start | bytes 3145736 | tf_op jit(solution)/shard_map/ppermute | solution.py:156
  206.8 31.1 %collective-permute-start.12 = (bf16[2,512,512]{2,1,0:T(8,128)(2,1)S(1)}, bf16[2,512,512]{2,1,0:T(8,128)(2,1)S(1)}, u32[]{:S(2)}, u32[]{:S(2)}) collective-permute-start(bf16[2,512,512]{2,1,0:T(8,128)(2,1)S(1)} %collective-permute-done.10), channel_id=1, source_target_pairs={{0,15},{1,0},{2,1},{3,2},{4,3},{5,4},{6,5},{7,6},{8,7},{9,8},{10,9... | collective-permute-start | bytes 3145736 | tf_op jit(solution)/shard_map/ppermute | solution.py:158
  223.0 15.3 %collective-permute-start.14 = (bf16[2,512,512]{2,1,0:T(8,128)(2,1)S(1)}, bf16[2,512,512]{2,1,0:T(8,128)(2,1)S(1)}, u32[]{:S(2)}, u32[]{:S(2)}) collective-permute-start(bf16[2,512,512]{2,1,0:T(8,128)(2,1)S(1)} %collective-permute-done.13), channel_id=1, source_target_pairs={{0,1},{1,2},{2,3},{3,4},{4,5},{5,6},{6,7},{7,8},{8,9},{9,10},{10,1... | collective-permute-start | bytes 3145736 | tf_op jit(solution)/shard_map/ppermute | solution.py:156
  238.3 1.9 copy-start.32
  238.3 1.9 copy-start.33
  238.7 1.7 copy-start.26
  238.8 2.1 copy-start.27
  239.8 1.5 copy-start.34
  239.8 1.8 copy-start.28
  239.8 1.8 copy-start.43
  240.9 9.9 %copy-start.4 = (bf16[1024,512]{1,0:T(8,128)(2,1)S(1)}, bf16[1024,512]{1,0:T(8,128)(2,1)}, u32[]{:S(2)}) copy-start(bf16[1024,512]{1,0:T(8,128)(2,1)} %all-gather.7.cloned.1.call-done) | copy-start | bytes 3145732
  241.3 11.5 %copy-start.1 = (bf16[1024,1024]{1,0:T(8,128)(2,1)S(1)}, bf16[1024,1024]{1,0:T(8,128)(2,1)}, u32[]{:S(2)}) copy-start(bf16[1024,1024]{1,0:T(8,128)(2,1)} %all-gather.5.cloned.1.call-done) | copy-start | bytes 6291460
  248.6 0.7 copy-start.15
  252.6 5.9 %copy-start.35 = (bf16[256,4,128]{2,1,0:T(4,128)(2,1)S(1)}, bf16[256,4,128]{2,1,0:T(4,128)(2,1)}, u32[]{:S(2)}) copy-start(bf16[256,4,128]{2,1,0:T(4,128)(2,1)} %convert_element_type.154) | copy-start | bytes 786436
  252.8 6.9 %copy-start.3 = (bf16[1024,512]{1,0:T(8,128)(2,1)S(1)}, bf16[1024,512]{1,0:T(8,128)(2,1)}, u32[]{:S(2)}) copy-start(bf16[1024,512]{1,0:T(8,128)(2,1)} %all-gather.9.cloned.1.call-done) | copy-start | bytes 3145732
  252.8 6.9 %copy-start.20 = (bf16[50,1024]{1,0:T(8,128)(2,1)S(1)}, bf16[50,1024]{1,0:T(8,128)(2,1)}, u32[]{:S(2)}) copy-start(bf16[50,1024]{1,0:T(8,128)(2,1)} %copy-done.19) | copy-start | bytes 307204
  257.5 0.7 copy-start.30
  257.6 2.1 copy-start.44
  258.6 1.0 copy-start.48
  268.9 1.2 copy-start.39
  270.1 0.7 copy-start.16
  276.0 4.8 %copy-start.8 = (f32[50,64]{1,0:T(8,128)S(1)}, f32[50,64]{1,0:T(8,128)}, u32[]{:S(2)}) copy-start(f32[50,64]{1,0:T(8,128)} %copy-done.7) | copy-start | bytes 38404
  276.0 4.8 %copy-start.11 = (f32[50,64]{1,0:T(8,128)S(1)}, f32[50,64]{1,0:T(8,128)}, u32[]{:S(2)}) copy-start(f32[50,64]{1,0:T(8,128)} %copy-done.10) | copy-start | bytes 38404
  276.0 6.1 %copy-start.36 = (bf16[256,4,128]{2,1,0:T(4,128)(2,1)S(1)}, bf16[256,4,128]{2,1,0:T(4,128)(2,1)}, u32[]{:S(2)}) copy-start(bf16[256,4,128]{2,1,0:T(4,128)(2,1)} %convert_element_type.154) | copy-start | bytes 786436
  277.1 6.1 %copy-start.22 = (bf16[50,1024]{1,0:T(8,128)(2,1)S(1)}, bf16[50,1024]{1,0:T(8,128)(2,1)}, u32[]{:S(2)}) copy-start(bf16[50,1024]{1,0:T(8,128)(2,1)} %copy-done.21) | copy-start | bytes 307204
  281.1 0.7 copy-start.31
  293.6 0.7 copy-start.14
  299.5 3.7 %copy-start.47 = (pred[256]{0:T(512)(128)(4,1)S(1)}, pred[256]{0:T(512)(128)(4,1)}, u32[]{:S(2)}) copy-start(pred[256]{0:T(512)(128)(4,1)} %copy-done.46) | copy-start | bytes 772
  299.5 4.1 %copy-start.9 = (f32[50,64]{1,0:T(8,128)S(1)}, f32[50,64]{1,0:T(8,128)}, u32[]{:S(2)}) copy-start(f32[50,64]{1,0:T(8,128)} %copy-done.7) | copy-start | bytes 38404
  299.5 4.1 %copy-start.12 = (f32[50,64]{1,0:T(8,128)S(1)}, f32[50,64]{1,0:T(8,128)}, u32[]{:S(2)}) copy-start(f32[50,64]{1,0:T(8,128)} %copy-done.10) | copy-start | bytes 38404
  299.5 5.5 %copy-start.37 = (bf16[256,4,128]{2,1,0:T(4,128)(2,1)S(1)}, bf16[256,4,128]{2,1,0:T(4,128)(2,1)}, u32[]{:S(2)}) copy-start(bf16[256,4,128]{2,1,0:T(4,128)(2,1)} %convert_element_type.154) | copy-start | bytes 786436
  300.6 5.4 %copy-start.18 = (bf16[50,1024]{1,0:T(8,128)(2,1)S(1)}, bf16[50,1024]{1,0:T(8,128)(2,1)}, u32[]{:S(2)}) copy-start(bf16[50,1024]{1,0:T(8,128)(2,1)} %copy-done.17) | copy-start | bytes 307204
  303.0 4.7 %copy-start.2 = (bf16[1024,1024]{1,0:T(8,128)(2,1)S(1)}, bf16[1024,1024]{1,0:T(8,128)(2,1)}, u32[]{:S(2)}) copy-start(bf16[1024,1024]{1,0:T(8,128)(2,1)} %all-gather.11.cloned.1.call-done) | copy-start | bytes 6291460
  304.6 4.7 %copy-start.24 = (bf16[1024,32]{0,1:T(8,128)(2,1)S(1)}, bf16[1024,32]{0,1:T(8,128)(2,1)}, u32[]{:S(2)}) copy-start(bf16[1024,32]{0,1:T(8,128)(2,1)} %param.27) | copy-start | bytes 196612
  304.6 4.7 %copy-start.42 = (f32[1024]{0:T(1024)S(1)}, f32[1024]{0:T(1024)}, u32[]{:S(2)}) copy-start(f32[1024]{0:T(1024)} %param.26) | copy-start | bytes 12292
  (4 other events, 2.6 us)
Sparse Core Ops, SparseCore 0:
  9.5 57.6 all-gather.6
  69.3 43.9 all-gather.8
  115.5 61.6 all-gather.4
  179.2 57.2 all-gather.10
